TPU v7x, 256 devices: a whole 4x4x8 slice. The times are simulated.
256 devices in a mesh: dp: 32 (over x, z), comp: 8 (over y, core).
Axes of the slice: x: 4, y: 4, z: 8, core: 2. Of those that a mesh axis runs over, the one named last changes fastest.
Arguments:
- embeddings: float32 [32768, 1024], P('dp'), may hold values from -6 to 6
- means: float32 [8192, 1024], P(('comp', 'dp')), may hold values from -2 to 2
- variances: float32 [8192, 1024], P(('comp', 'dp')), may hold values from 0.7 to 1.4
- log_weights: float32 [8192], P(('comp', 'dp')), may hold values from -2 to 0
Outputs:
- new_means: float32 [8192, 1024], P(('comp', 'dp'))
- new_variances: float32 [8192, 1024], P(('comp', 'dp'))
- new_weights: float32 [8192], P(('comp', 'dp'))
- row_loglik: float32 [32768], P('dp')
All inputs are finite; a program needn't handle non-finite values.
Results may differ from a plain program's by a relative error of at most 0.00045.
Values sent between devices are 32-bit elements; how exact they have to be, the bound alone decides.
A program may use at most 128 MiB of HBM per device.

v0:
```python
import jax
import jax.numpy as jnp
from jax import lax
from jax.sharding import PartitionSpec as P

circle_log = 1.8378770664093453


def component_terms(means, variances, log_weights):
    precision = 1.0 / variances
    scaled = means * precision
    width = means.shape[1]
    offset = (
        log_weights
        - 0.5 * jnp.sum(jnp.log(variances), axis=1)
        - 0.5 * jnp.sum(means * scaled, axis=1)
        - 0.5 * width * circle_log
    )
    return (precision, scaled, offset)


def row_scores(block, squares, precision, scaled, offset):
    highest = lax.Precision.HIGHEST
    quad = jnp.dot(squares, precision.T, precision=highest, preferred_element_type=jnp.float32)
    cross = jnp.dot(block, scaled.T, precision=highest, preferred_element_type=jnp.float32)
    return offset[None, :] + cross - 0.5 * quad


def weighted_sum(resp, values):
    return lax.dot_general(
        resp,
        values,
        (((0,), (0,)), ((), ())),
        precision=lax.Precision.HIGHEST,
        preferred_element_type=jnp.float32,
    )


def per_device(embeddings, means, variances, log_weights):
    squares = embeddings * embeddings
    precision, scaled, offset = component_terms(
        lax.all_gather(means, "dp", axis=0, tiled=True),
        lax.all_gather(variances, "dp", axis=0, tiled=True),
        lax.all_gather(log_weights, "dp", axis=0, tiled=True),
    )
    scores = row_scores(embeddings, squares, precision, scaled, offset)
    local_peak = jnp.max(scores, axis=1)
    peak = lax.pmax(local_peak, "comp")
    total = lax.psum(jnp.sum(jnp.exp(scores - peak[:, None]), axis=1), "comp")
    row_loglik = peak + jnp.log(total)
    resp = jnp.exp(scores - row_loglik[:, None])
    summed = lax.psum_scatter(
        jnp.concatenate([weighted_sum(resp, embeddings), weighted_sum(resp, squares)], axis=1),
        "dp",
        scatter_dimension=0,
        tiled=True,
    )
    counts = lax.psum_scatter(jnp.sum(resp, axis=0), "dp", scatter_dimension=0, tiled=True)
    width = embeddings.shape[1]
    first = summed[:, :width]
    second = summed[:, width:]
    denom = (counts + 1.0)[:, None]
    new_means = (first + means) / denom
    new_variances = (second + variances + means * means) / denom - new_means * new_means
    new_weights = counts / (embeddings.shape[0] * lax.axis_size("dp"))
    return (new_means, new_variances, new_weights, row_loglik)


def solution(mesh):
    return jax.shard_map(
        per_device,
        mesh=mesh,
        in_specs=(
            P("dp", None),
            P(("comp", "dp"), None),
            P(("comp", "dp"), None),
            P(("comp", "dp")),
        ),
        out_specs=(P(("comp", "dp"), None), P(("comp", "dp"), None), P(("comp", "dp")), P("dp")),
        check_vma=False,
    )
```

profile of v0, /device:TPU:8, one launch (start us, length us, event | category | flops | bytes accessed | tf_op | source)
XLA Modules:
  0.0 516.7 jit_solution(10036778705342761832)
XLA Ops:
  7.2 0.0 all-gather.5.cloned.1.call-start
  7.2 0.7 all-gather.5.cloned.1.call-update
  7.9 0.0 all-gather.3.cloned.1.call-start
  7.9 0.7 all-gather.3.cloned.1.call-update
  8.6 0.0 reduce-scatter.4.cloned.1.call-start
  8.7 1.3 fusion.17
  10.7 0.9 dynamic-update-slice
  11.6 78.0 %all-reduce = f32[1024]{0:T(1024)S(1)} all-reduce(f32[1024]{0:T(1024)S(1)} %dynamic-update-slice), channel_id=1, replica_groups=mesh['dp'=32,'comp'=8] {'dp'}, use_global_device_ids=true, to_apply=%add | all-reduce | flops 1024 | bytes 8192
  89.6 5.7 %all-gather.5.cloned.1.call-done = f32[1024,1024]{1,0:T(8,128)} async-done(((f32[32,1024]{1,0:T(8,128)}), f32[1024,1024]{1,0:T(8,128)}) %all-gather.5.cloned.1.call-update) | async-done | bytes 4194320 | tf_op jit(solution)/shard_map/all_gather | solution.py:42
  95.3 81.7 %all-gather.3.cloned.1.call-done = f32[1024,1024]{1,0:T(8,128)} async-done(((f32[32,1024]{1,0:T(8,128)}), f32[1024,1024]{1,0:T(8,128)}) %all-gather.3.cloned.1.call-update) | async-done | bytes 4194320 | tf_op jit(solution)/shard_map/all_gather | solution.py:43
  177.0 0.0 copy-start.2
  177.0 0.0 copy-start.6
  177.0 5.1 log_reduce_fusion
  182.1 0.0 copy-done.2
  182.1 0.7 copy-done.6
  182.9 0.0 copy-start.1
  182.9 13.6 %fusion.2 = f32[1024,1024]{0,1:T(8,128)S(1)} fusion(f32[1024,1024]{1,0:T(8,128)S(1)} %copy-done.6, f32[1024,1024]{1,0:T(8,128)S(1)} %copy-done.2), kind=kOutput, calls=%fused_computation.8 | convolution fusion | flops 12886999040 | bytes 12582912 | tf_op jit(solution)/shard_map/dot_general | solution.py:24
  196.4 0.0 copy-done.1
  196.4 15.2 %fusion.18 = (f32[1024]{0:T(1024)S(1)}, f32[1024,1024]{0,1:T(8,128)}) fusion(f32[1024,1024]{0,1:T(8,128)S(1)} %fusion.2, f32[1024,1024]{1,0:T(8,128)S(1)} %copy-done.6, f32[1024,1024]{1,0:T(8,128)S(1)} %copy-done.1, f32[1024,1024]{1,0:T(8,128)S(1)} %copy-done.2, f32[1024]{0:T(1024)S(1)} %subtract_add_fusion), kind=kOutput, calls=%fused_computation.28 | convolution fusion | flops 12891192320 | bytes 20979712 | tf_op jit(solution)/shard_map/dot_general | solution.py:25
  211.7 10.0 %pmax.7 = f32[1024]{0:T(1024)S(1)} all-reduce(f32[1024]{0:T(1024)S(1)} %get-tuple-element.20), channel_id=1, replica_groups=mesh['dp'=32,'comp'=8] {'comp'}, use_global_device_ids=true, to_apply=%region_3.0 | all-reduce | flops 1024 | bytes 8192 | tf_op jit(solution)/shard_map/pmax | solution.py:48
  221.6 2.8 exponential_reduce_fusion
  224.4 12.4 %psum.7 = f32[1024]{0:T(1024)S(1)} all-reduce(f32[1024]{0:T(1024)S(1)} %exponential_reduce_fusion), channel_id=1, replica_groups=mesh['dp'=32,'comp'=8] {'comp'}, use_global_device_ids=true, to_apply=%region_5.0 | all-reduce | flops 1024 | bytes 8192 | tf_op jit(solution)/shard_map/psum | solution.py:49
  236.9 0.0 copy-start.5
  236.9 0.0 copy-start
  236.9 0.0 copy-start.7
  236.9 17.7 %fusion = f32[1024,1024]{0,1:T(8,128)S(1)} fusion(f32[1024,1024]{1,0:T(8,128)} %param.4, f32[1024,1024]{0,1:T(8,128)} %get-tuple-element.21, f32[1024]{0:T(1024)S(1)} %log_add_fusion), kind=kOutput, calls=%fused_computation.6 | convolution fusion | flops 12886999040 | bytes 12587008 | tf_op jit(solution)/shard_map/dot_general | solution.py:30
  254.6 0.0 copy-done
  254.6 0.0 copy-done.7
  254.6 13.8 %fusion.7 = f32[1024,1024]{0,1:T(8,128)S(1)} fusion(f32[1024,1024]{1,0:T(8,128)S(1)} %copy-done.7, f32[1024,1024]{0,1:T(8,128)S(1)} %copy-done, f32[1024]{0:T(1024)S(1)} %log_add_fusion), kind=kOutput, calls=%fused_computation.13 | convolution fusion | flops 12885950464 | bytes 12587008 | tf_op jit(solution)/shard_map/dot_general | solution.py:30
  268.5 4.1 pad_maximum_fusion
  272.5 9.1 %copy.22 = f32[1024,2048]{1,0:T(8,128)} copy(f32[1024,2048]{0,1:T(8,128)} %pad_maximum_fusion) | data formatting | bytes 16777216
  281.7 0.0 reduce-scatter.4.cloned.1.call-update
  281.7 0.0 copy-start.3
  281.7 0.0 copy-start.4
  282.4 0.0 copy-done.5
  282.4 2.8 fusion.6
  285.2 72.8 %all-reduce.1 = f32[1024]{0:T(1024)S(1)} all-reduce(f32[1024]{0:T(1024)S(1)} %fusion.6), channel_id=3, replica_groups=mesh['dp'=32,'comp'=8] {'dp'}, use_global_device_ids=true, to_apply=%region_8.0.clone | all-reduce | flops 1024 | bytes 8192
  358.0 0.6 broadcast_multiply_fusion
  358.6 149.4 %reduce-scatter.4.cloned.1.call-done = f32[32,2048]{1,0:T(8,128)} async-done(((f32[1024,2048]{1,0:T(8,128)}), f32[32,2048]{1,0:T(8,128)}) %reduce-scatter.4.cloned.1.call-update) | async-done | bytes 262160 | tf_op jit(solution)/shard_map/reduce_scatter | solution.py:52
  507.9 0.0 copy-done.3
  507.9 0.0 copy-done.4
  507.9 1.8 fusion.14
  (3 shorter events, 0.0 us)
Async XLA Ops:
  7.2 88.1 %all-gather.5.cloned.1.call-start = ((), (), s32[]{:S(2)}) async-start(), calls=%async_computation.2 | async-start | bytes 4325376 | tf_op jit(solution)/shard_map/all_gather | solution.py:42
  7.9 169.1 %all-gather.3.cloned.1.call-start = ((), (), s32[]{:S(2)}) async-start(), calls=%async_computation.1 | async-start | bytes 4325376 | tf_op jit(solution)/shard_map/all_gather | solution.py:43
  8.6 499.3 %reduce-scatter.4.cloned.1.call-start = ((), (), s32[]{:S(2)}) async-start(), calls=%async_computation.3 | async-start | bytes 8650752 | tf_op jit(solution)/shard_map/reduce_scatter | solution.py:52
  177.0 5.2 copy-start.2
  177.0 5.9 %copy-start.6 = (f32[1024,1024]{1,0:T(8,128)S(1)}, f32[1024,1024]{1,0:T(8,128)}, u32[]{:S(2)}) copy-start(f32[1024,1024]{1,0:T(8,128)} %param.4) | copy-start | bytes 12582916
  182.9 13.6 %copy-start.1 = (f32[1024,1024]{1,0:T(8,128)S(1)}, f32[1024,1024]{1,0:T(8,128)}, u32[]{:S(2)}) copy-start(f32[1024,1024]{1,0:T(8,128)} %all-gather.5.cloned.1.call-done) | copy-start | bytes 12582916
  236.9 45.5 %copy-start.5 = (f32[1024]{0:T(1024)}, f32[1024]{0:T(1024)S(1)}, u32[]{:S(2)}) copy-start(f32[1024]{0:T(1024)S(1)} %log_add_fusion) | copy-start | bytes 12292
  236.9 17.7 %copy-start = (f32[1024,1024]{0,1:T(8,128)S(1)}, f32[1024,1024]{0,1:T(8,128)}, u32[]{:S(2)}) copy-start(f32[1024,1024]{0,1:T(8,128)} %get-tuple-element.21) | copy-start | bytes 12582916
  236.9 17.7 %copy-start.7 = (f32[1024,1024]{1,0:T(8,128)S(1)}, f32[1024,1024]{1,0:T(8,128)}, u32[]{:S(2)}) copy-start(f32[1024,1024]{1,0:T(8,128)} %param.4) | copy-start | bytes 12582916
  281.7 226.3 %copy-start.3 = (f32[32,1024]{1,0:T(8,128)S(1)}, f32[32,1024]{1,0:T(8,128)}, u32[]{:S(2)}) copy-start(f32[32,1024]{1,0:T(8,128)} %param.6) | copy-start | bytes 393220
  281.7 226.2 %copy-start.4 = (f32[32,1024]{1,0:T(8,128)S(1)}, f32[32,1024]{1,0:T(8,128)}, u32[]{:S(2)}) copy-start(f32[32,1024]{1,0:T(8,128)} %param.5) | copy-start | bytes 393220
Sparse Core Ops, SparseCore 0:
  10.6 84.6 all-gather.4
  97.9 79.0 all-gather.2
  281.8 226.0 reduce-scatter.3
where the time goes:
time: 526 us; the launch traced here: 517 us
  waiting for transfers between devices  238 us (45%)
  blocking collectives  173 us (33%)
  matrix products  60.3 us (11%)
  other arithmetic  17.2 us (3%)
  between operations  15.7 us (3%)
  local copies, waits for them, and re-layouts  12.1 us (2%)
    unnamed x2, blocking collectives  151 us
    reduce_scatter x1, waiting for transfers between devices, per_device(): lax.psum_scatter(jnp.concatenate([weighted_sum(resp, embeddings), weighte...  149 us
    all_gather x1, waiting for transfers between devices, per_device(): lax.all_gather(variances, 'dp', axis=0, tiled=True)  81.7 us
    dot_general x2, matrix products, weighted_sum(): lax.dot_general(resp, values, (((0,), (0,)), ((), ())), precision=lax.Pre...  31.5 us
    dot_general x1, matrix products, row_scores(): jnp.dot(block, scaled.T, precision=highest, preferred_element_type=jnp.fl...  15.2 us
    dot_general x1, matrix products, row_scores(): jnp.dot(squares, precision.T, precision=highest, preferred_element_type=j...  13.6 us
    psum x1, blocking collectives, per_device(): total = lax.psum(jnp.sum(jnp.exp(scores - peak[:, None]), axis=1), 'comp')  12.4 us
    unnamed x20, local copies, waits for them, and re-layouts  12.1 us
  transfers between devices with their start and end apart: 3, of which 3 were waited for; matrix products, arithmetic and copies ran while one was open for 1% of the time, Pallas kernels for 0%

commit v1 on v0

v1 whole, which is shorter than its diff:
```python
import functools

import jax
import jax.numpy as jnp
from jax import lax
from jax.experimental import pallas as pl
from jax.experimental.pallas import tpu as pltpu
from jax.sharding import PartitionSpec as P

circle_log = 1.8378770664093453
MESH = pl.DeviceIdType.MESH
NX = 4
LAG = 1.6
UNIT = 2.8


def sign(v):
    return (v > 0) - (v < 0)


def canon(d, n):
    d = d % n
    return d if d <= n // 2 else d - n


def hops_on(d, n):
    out = []
    for way in (1, -1):
        if d != 0 and (d > 0) == (way > 0):
            continue
        if abs(d) == n // 2:
            continue
        new = d - way
        if abs(new) < n // 2:
            out.append((way, new, None))
        elif abs(new) == n // 2:
            out.append((way, n // 2, 0 if way > 0 else 1))
    return out


def axes_of(stream):
    return ("x", "z") if stream == 0 else ("z", "x")


def gather_sends(stream, df, ds, nf, ns):
    first, second = axes_of(stream)
    out = []
    if ds == 0:
        out += [(first, way, (d, 0, half)) for way, d, half in hops_on(df, nf)]
    out += [(second, way, (df, d, half)) for way, d, half in hops_on(ds, ns)]
    return out


def gather_plan(nx, nz):
    size = {"x": nx, "z": nz}
    free, arrivals, plan = {}, [], []
    t = 0.0
    halves, left = {}, {(s, dx): nz for s in (0, 1) for dx in range(nx)}
    ready, dots = [], 0

    def available(stream, df, ds):
        nonlocal t
        first, second = axes_of(stream)
        for axis, way, slot in gather_sends(stream, df, ds, size[first], size[second]):
            work = (1.0 if stream == 0 else 1.125) * UNIT * (0.5 if slot[2] is not None else 1.0)
            start = max(t, free.get((axis, way), 0.0))
            free[(axis, way)] = start + work
            arrivals.append((start + work + LAG, stream, slot))
            plan.append(("send", stream, (df, ds), axis, way, slot))
        dx = (df if stream == 0 else ds) % nx
        left[(stream, dx)] -= 1
        if left[(stream, dx)] == 0:
            ready.append((stream, dx))

    available(0, 0, 0)
    available(1, 0, 0)
    plan.append(("split",))
    t += 3.0
    while arrivals or ready:
        arrivals.sort(key=lambda a: (a[0], a[1], str(a[2])))
        if arrivals and arrivals[0][0] <= t or not ready:
            when, stream, (df, ds, half) = arrivals.pop(0)
            t = max(t, when)
            plan.append(("recv", stream, (df, ds, half)))
            if half is not None:
                halves[(stream, df, ds)] = halves.get((stream, df, ds), 0) + 1
                if halves[(stream, df, ds)] < 2:
                    continue
            available(stream, df, ds)
        else:
            stream, dx = ready.pop(0)
            plan.append(("dot", stream, dx))
            t += 2.2
    return plan


def reduce_inputs(stream, df, ds, nf, ns):
    def along(d, n):
        if d == 0:
            return [(1, None), (-1, None)] if n > 2 else []
        if abs(d) == n // 2:
            return []
        far = d + sign(d)
        if abs(far) == n // 2:
            return [(n // 2, 0 if d > 0 else 1)]
        return [(far, None)]

    out = [(df, d, half) for d, half in along(ds, ns)]
    if ds == 0:
        out += [(d, 0, half) for d, half in along(df, nf)]
    return out


def reduce_sends(stream, df, ds, nf, ns):
    first, second = axes_of(stream)
    axis, d, n = (second, ds, ns) if ds != 0 else (first, df, nf)
    if d == 0:
        return []
    if abs(d) == n // 2:
        return [(axis, 1, (df, ds, 0)), (axis, -1, (df, ds, 1))]
    return [(axis, sign(d), (df, ds, None))]


def reduce_plan(nx, nz):
    size = {"x": nx, "z": nz}
    free, arrivals, plan = {}, [], []
    t = 0.0
    groups = sorted(range(nx), key=lambda dx: (-abs(canon(dx, nx)), dx))
    done, landed = set(), set()
    waiting = []
    for stream in (0, 1):
        first, second = axes_of(stream)
        for f in range(size[first]):
            for s in range(size[second]):
                waiting.append((stream, canon(f, size[first]), canon(s, size[second])))

    def is_ready(item):
        stream, df, ds = item
        first, second = axes_of(stream)
        if (df if stream == 0 else ds) % nx not in done:
            return False
        needs = reduce_inputs(stream, df, ds, size[first], size[second])
        return all((stream, n) in landed for n in needs)

    while waiting:
        for a in [a for a in arrivals if a[0] <= t]:
            arrivals.remove(a)
            landed.add(a[1:])
        ready = sorted(
            (w for w in waiting if is_ready(w)),
            key=lambda w: (-abs(w[1]) - abs(w[2]), w),
        )
        if ready:
            item = ready[0]
            waiting.remove(item)
            stream, df, ds = item
            first, second = axes_of(stream)
            plan.append(("sum", stream, (df, ds)))
            t += 0.15
            for axis, way, slot in reduce_sends(stream, df, ds, size[first], size[second]):
                work = (1.0 if stream == 0 else 1.125) * UNIT * (0.5 if slot[2] is not None else 1.0)
                start = max(t, free.get((axis, way), 0.0))
                free[(axis, way)] = start + work
                arrivals.append((start + work + LAG, stream, slot))
        elif groups:
            dx = groups.pop(0)
            plan.append(("moments", dx))
            t += 4.5
            done.add(dx)
        else:
            t = min(a[0] for a in arrivals)
    return plan


class Place:
    def __init__(self, nx, nz):
        self.nx, self.nz = nx, nz
        me = lax.axis_index("dp")
        self.x, self.z = me // nz, me % nz

    def block(self, dx, dz):
        return ((self.x + dx) % self.nx) * self.nz + (self.z + dz) % self.nz

    def of(self, stream, df, ds):
        return self.block(df, ds) if stream == 0 else self.block(ds, df)

    def group(self, dx):
        return (self.x + dx) % self.nx

    def neighbour(self, axis, way):
        dp = self.block(way, 0) if axis == "x" else self.block(0, way)
        return {"dp": dp}

    def slot(self, stream, slot):
        df, ds, half = slot
        nf, ns = (self.nx, self.nz) if stream == 0 else (self.nz, self.nx)
        return ((df % nf) * ns + ds % ns) * 2 + (half or 0)


def part(ref, index, half):
    rows = ref.shape[1]
    if half is None:
        return ref.at[index]
    return ref.at[index, pl.ds(half * (rows // 2), rows // 2)]


def greet(place, comps):
    barrier = pltpu.get_barrier_semaphore()
    count = 4
    for axis in ("x", "z"):
        for way in (1, -1):
            pl.semaphore_signal(barrier, inc=1, device_id=place.neighbour(axis, way), device_id_type=MESH)
    if comps > 1:
        mine = lax.axis_index("comp")
        for k in range(1, comps):
            pl.semaphore_signal(barrier, inc=1, device_id={"comp": (mine + k) % comps}, device_id_type=MESH)
        count += comps - 1
    pl.semaphore_wait(barrier, count)


def split(x):
    high = x.astype(jnp.bfloat16)
    return high, (x - high.astype(jnp.float32)).astype(jnp.bfloat16)


def dot_nt(a, b):
    return lax.dot_general(a, b, (((1,), (1,)), ((), ())), preferred_element_type=jnp.float32)


def dot_nn(a, b):
    return jnp.dot(a, b, preferred_element_type=jnp.float32)


def split_rows(x_ref, xh, xl, qh, ql):
    rows = x_ref.shape[0]
    tile = min(64, rows)

    @pl.loop(0, rows // tile)
    def _(i):
        at = pl.ds(pl.multiple_of(i * tile, tile), tile)
        x = x_ref[at, :]
        xh[at, :], xl[at, :] = split(x)
        qh[at, :], ql[at, :] = split(x * x)


def scores_kernel(
    nx, nz, comps, x_ref, means_ref, var_ref, logw_ref, scores_ref, norm_ref,
    scaled, prec, xh, xl, qh, ql, ph, plo, stat, send_a, recv_a, send_b, recv_b, stat_send, stat_recv,
):
    place = Place(nx, nz)
    rows, width = x_ref.shape
    size = means_ref.shape[0]
    group = nz * size
    own = place.block(0, 0)
    variances = var_ref[...]
    means = means_ref[...]
    p = 1.0 / variances
    sc = means * p
    offset = (
        logw_ref[...]
        - 0.5 * jnp.sum(jnp.log(variances), axis=1, keepdims=True)
        - 0.5 * jnp.sum(means * sc, axis=1, keepdims=True)
    )
    scaled[own] = sc
    prec[own, :, 0:width] = -0.5 * (p - 1.0)
    prec[own, :, width : width + 128] = jnp.broadcast_to(offset, (size, 128))
    greet(place, comps)

    bufs, sends, recvs = (scaled, prec), (send_a, send_b), (recv_a, recv_b)
    started = []
    seen = set()
    first_stat = True
    mine = lax.axis_index("comp")
    tile = min(256, rows)

    def copy(stream, offs, axis, way, slot):
        index = place.of(stream, *offs)
        n = place.slot(stream, slot)
        ref = part(bufs[stream], index, slot[2])
        return pltpu.make_async_remote_copy(
            src_ref=ref,
            dst_ref=ref,
            send_sem=sends[stream].at[n],
            recv_sem=recvs[stream].at[n],
            device_id=place.neighbour(axis, way),
            device_id_type=MESH,
        )

    for op in gather_plan(nx, nz):
        if op[0] == "send":
            c = copy(*op[1:])
            c.start()
            started.append(c)
        elif op[0] == "recv":
            _, stream, slot = op
            copy(stream, slot[:2], "x", 1, slot).wait_recv()
        elif op[0] == "split":
            split_rows(x_ref, xh, xl, qh, ql)
        else:
            _, stream, dx = op
            g = place.group(dx)
            blocks = pl.ds(pl.multiple_of(g * nz, nz), nz)
            at = pl.ds(pl.multiple_of(g * group, group), group)
            values = bufs[stream][blocks, :, 0:width].reshape(group, width)
            ph[...], plo[...] = split(values)
            high, low = (xh, xl) if stream == 0 else (qh, ql)
            last = dx in seen
            seen.add(dx)
            start = last and first_stat
            if last:
                first_stat = False

            @pl.loop(0, rows // tile)
            def _(i):
                n = pl.ds(pl.multiple_of(i * tile, tile), tile)
                s = dot_nt(ph[...], high[n, :]) + dot_nt(ph[...], low[n, :]) + dot_nt(plo[...], high[n, :])
                if not last:
                    scores_ref[at, n] = s
                    return
                off = prec[blocks, :, width : width + 128].reshape(group, 128)[:, 0:1]
                s = s + scores_ref[at, n] + off
                scores_ref[at, n] = s
                peak = jnp.max(s, axis=0, keepdims=True)
                if start:
                    stat[mine, 0:1, n] = peak
                    stat[mine, 1:2, n] = jnp.sum(jnp.exp(s - peak), axis=0, keepdims=True)
                else:
                    before = stat[mine, 0:1, n]
                    now = jnp.maximum(before, peak)
                    stat[mine, 1:2, n] = stat[mine, 1:2, n] * jnp.exp(before - now) + jnp.sum(
                        jnp.exp(s - now), axis=0, keepdims=True
                    )
                    stat[mine, 0:1, n] = now

    for k in range(1, comps):
        c = pltpu.make_async_remote_copy(
            src_ref=stat.at[mine],
            dst_ref=stat.at[mine],
            send_sem=stat_send.at[k],
            recv_sem=stat_recv.at[k],
            device_id={"comp": (mine + k) % comps},
            device_id_type=MESH,
        )
        c.start()
        started.append(c)
    ones = jnp.ones((8, width), jnp.bfloat16)

    @pl.loop(0, rows // tile)
    def _(i):
        n = pl.ds(pl.multiple_of(i * tile, tile), tile)
        norm_ref[:, n] = 0.5 * (dot_nt(ones, qh[n, :]) + dot_nt(ones, ql[n, :]))

    for k in range(1, comps):
        source = (mine - k + comps) % comps
        pltpu.make_async_remote_copy(
            src_ref=stat.at[source],
            dst_ref=stat.at[source],
            send_sem=stat_send.at[k],
            recv_sem=stat_recv.at[k],
            device_id={"comp": source},
            device_id_type=MESH,
        ).wait_recv()
    peak = stat[0, 0:1, :]
    for c in range(1, comps):
        peak = jnp.maximum(peak, stat[c, 0:1, :])
    total = jnp.zeros_like(peak)
    for c in range(comps):
        total = total + stat[c, 1:2, :] * jnp.exp(stat[c, 0:1, :] - peak)
    norm = peak + jnp.log(total)
    norm_ref[1:2, :] = norm - norm_ref[1:2, :] - 0.5 * width * circle_log
    norm_ref[0:1, :] = norm
    for c in started:
        c.wait_send()


def moments_kernel(
    nx, nz, x_ref, scores_ref, norm_ref, first_ref, second_ref,
    xh, xl, qh, ql, rh, rl, sum_a, sum_b, land_a, land_b, send_a, recv_a, send_b, recv_b,
):
    place = Place(nx, nz)
    rows, width = x_ref.shape
    size = first_ref.shape[0]
    group = nz * size
    split_rows(x_ref, xh, xl, qh, ql)
    greet(place, 1)
    sums, lands, sends, recvs = (sum_a, sum_b), (land_a, land_b), (send_a, send_b), (recv_a, recv_b)
    started = []

    def copy(stream, axis, way, slot):
        df, ds, half = slot
        n = place.slot(stream, slot)
        return pltpu.make_async_remote_copy(
            src_ref=part(sums[stream], place.of(stream, df, ds), half),
            dst_ref=part(lands[stream], n // 2, half),
            send_sem=sends[stream].at[n],
            recv_sem=recvs[stream].at[n],
            device_id=place.neighbour(axis, way),
            device_id_type=MESH,
        )

    for op in reduce_plan(nx, nz):
        if op[0] == "moments":
            g = place.group(op[1])
            base = g * nz
            few = max(1, nz // 4)

            @pl.loop(0, nz // few)
            def _(i):
                chunk = few * size
                at = pl.ds(pl.multiple_of(g * group + i * chunk, chunk), chunk)
                here = pl.ds(pl.multiple_of(i * chunk, chunk), chunk)
                r = jnp.exp(scores_ref[at, :] - norm_ref[0:1, :])
                counts = jnp.sum(r, axis=1, keepdims=True)
                rh[here, :], rl[here, :] = split(r)
                sum_b[pl.ds(base + i * few, few), :, width : width + 128] = jnp.broadcast_to(
                    counts, (chunk, 128)
                ).reshape(few, size, 128)

            blocks = pl.ds(pl.multiple_of(base, nz), nz)
            tile = min(256, width)

            @pl.loop(0, width // tile)
            def _(i):
                d = pl.ds(pl.multiple_of(i * tile, tile), tile)
                a = dot_nn(rh[...], xh[:, d]) + dot_nn(rh[...], xl[:, d]) + dot_nn(rl[...], xh[:, d])
                sum_a[blocks, :, d] = a.reshape(nz, size, tile)
                b = dot_nn(rh[...], qh[:, d]) + dot_nn(rh[...], ql[:, d]) + dot_nn(rl[...], qh[:, d])
                sum_b[blocks, :, d] = b.reshape(nz, size, tile)
            continue
        _, stream, (df, ds) = op
        nf, ns = (nx, nz) if stream == 0 else (nz, nx)
        index = place.of(stream, df, ds)
        whole, cut = [], []
        for slot in reduce_inputs(stream, df, ds, nf, ns):
            copy(stream, "x", 1, slot).wait_recv()
            (whole if slot[2] is None else cut).append(slot)
        out = sums[stream]
        final = (df, ds) == (0, 0)
        if whole:
            v = out[index]
            for slot in whole:
                v = v + lands[stream][place.slot(stream, slot) // 2]
            if final:
                (first_ref, second_ref)[stream][...] = v
            else:
                out[index] = v
        for slot in cut:
            at = pl.ds(slot[2] * (size // 2), size // 2)
            out[index, at] = out[index, at] + lands[stream][place.slot(stream, slot) // 2, at]
        for axis, way, slot in reduce_sends(stream, df, ds, nf, ns):
            c = copy(stream, axis, way, slot)
            c.start()
            started.append(c)
    for c in started:
        c.wait_send()


def per_device(nx, nz, comps, x, means, variances, log_weights):
    rows, width = x.shape
    size = means.shape[0]
    count = nx * nz
    local = count * size
    vmem = pl.BlockSpec(memory_space=pltpu.VMEM)
    f32, bf16 = jnp.float32, jnp.bfloat16
    parts = [pltpu.VMEM((rows, width), bf16)] * 4
    sems = [pltpu.SemaphoreType.DMA((2 * count,))] * 4
    scores, norm = pl.pallas_call(
        functools.partial(scores_kernel, nx, nz, comps),
        out_shape=(jax.ShapeDtypeStruct((local, rows), f32), jax.ShapeDtypeStruct((8, rows), f32)),
        in_specs=[vmem] * 4,
        out_specs=(vmem, vmem),
        scratch_shapes=[
            pltpu.VMEM((count, size, width), f32),
            pltpu.VMEM((count, size, width + 128), f32),
            *parts,
            pltpu.VMEM((nz * size, width), bf16),
            pltpu.VMEM((nz * size, width), bf16),
            pltpu.VMEM((comps, 8, rows), f32),
            *sems,
            pltpu.SemaphoreType.DMA((comps,)),
            pltpu.SemaphoreType.DMA((comps,)),
        ],
        compiler_params=pltpu.CompilerParams(
            collective_id=0, has_side_effects=True, vmem_limit_bytes=56 << 20
        ),
        name="scores",
    )(x, means, variances, log_weights[:, None])
    first, second = pl.pallas_call(
        functools.partial(moments_kernel, nx, nz),
        out_shape=(jax.ShapeDtypeStruct((size, width), f32), jax.ShapeDtypeStruct((size, width + 128), f32)),
        in_specs=[vmem] * 3,
        out_specs=(vmem, vmem),
        scratch_shapes=[
            *parts,
            pltpu.VMEM((nz * size, rows), bf16),
            pltpu.VMEM((nz * size, rows), bf16),
            pltpu.VMEM((count, size, width), f32),
            pltpu.VMEM((count, size, width + 128), f32),
            pltpu.VMEM((count, size, width), f32),
            pltpu.VMEM((count, size, width + 128), f32),
            *sems,
        ],
        compiler_params=pltpu.CompilerParams(
            collective_id=1, has_side_effects=True, vmem_limit_bytes=56 << 20
        ),
        name="moments",
    )(x, scores, norm)
    counts = second[:, width]
    denom = (counts + 1.0)[:, None]
    new_means = (first + means) / denom
    new_variances = (second[:, :width] + variances + means * means) / denom - new_means * new_means
    new_weights = counts / (rows * count)
    return (new_means, new_variances, new_weights, norm[1])


def solution(mesh):
    count, comps = mesh.shape["dp"], mesh.shape["comp"]
    return jax.shard_map(
        functools.partial(per_device, NX, count // NX, comps),
        mesh=mesh,
        in_specs=(
            P("dp", None),
            P(("comp", "dp"), None),
            P(("comp", "dp"), None),
            P(("comp", "dp")),
        ),
        out_specs=(P(("comp", "dp"), None), P(("comp", "dp"), None), P(("comp", "dp")), P("dp")),
        check_vma=False,
    )
```

time: 526 us -> 165 us (0.31); the launches traced: 517 us -> 164 us
  waiting for transfers between devices: 238 us -> 0 us
  blocking collectives: 173 us -> 0 us
  Pallas kernels: 0 us -> 158 us
  matrix products: 60.3 us -> 0 us
  between operations: 15.7 us -> 0.66 us
  other arithmetic: 17.2 us -> 3.1 us
  local copies, waits for them, and re-layouts: 12.1 us -> 2.71 us
    pallas_call x0 -> x2, Pallas kernels: none -> 158 us  [the longest x1 85 us: per_device(): pl.pallas_call(functools.partial(scores_kernel, nx, nz, comps), out_shape...]
    unnamed x2 -> x0, blocking collectives: 151 us -> none
    reduce_scatter x1 -> x0, waiting for transfers between devices: 149 us -> none  [per_device(): lax.psum_scatter(jnp.concatenate([weighted_sum(resp, embeddings), weighte...]
    all_gather x2 -> x0, waiting for transfers between devices: 87.3 us -> none  [the longest x1 81.7 us: per_device(): lax.all_gather(variances, 'dp', axis=0, tiled=True)]
    dot_general x4 -> x0, matrix products: 60.3 us -> none  [the longest x2 31.5 us: weighted_sum(): lax.dot_general(resp, values, (((0,), (0,)), ((), ())), precision=lax.Pre...]
    psum x1 -> x0, blocking collectives: 12.4 us -> none  [per_device(): total = lax.psum(jnp.sum(jnp.exp(scores - peak[:, None]), axis=1), 'comp')]
    unnamed x20 -> x4, local copies, waits for them, and re-layouts: 12.1 us -> 0.01 us
    reduce_sum x3 -> x0, other arithmetic: 10.8 us -> none  [the longest x1 5.15 us: component_terms(): jnp.sum(jnp.log(variances), axis=1)]
  transfers between devices with their start and end apart: 3 -> 0, of which waited for: 3 -> 0; matrix products, arithmetic and copies ran while one was open for 1% -> 0% of each run, Pallas kernels for 0% -> 0%
where the time goes in v1:
time: 165 us; the launch traced here: 164 us
  Pallas kernels  158 us (96%)
  other arithmetic  3.1 us (2%)
  local copies, waits for them, and re-layouts  2.71 us (2%)
    pallas_call x1, Pallas kernels, per_device(): pl.pallas_call(functools.partial(scores_kernel, nx, nz, comps), out_shape...  85 us
    pallas_call x1, Pallas kernels, per_device(): pl.pallas_call(functools.partial(moments_kernel, nx, nz), out_shape=(jax....  73.1 us

profile of v1, /device:TPU:8, one launch (start us, length us, event | category | flops | bytes accessed | tf_op | source)
XLA Modules:
  0.0 164.5 jit_solution(3730307356219436392)
XLA Ops:
  0.6 1.3 copy.9.logw_ref
  2.0 85.0 %scores.1 = (f32[1024,1024]{1,0:T(8,128)}, f32[8,1024]{1,0:T(8,128)}) custom-call(f32[1024,1024]{1,0:T(8,128)} %x_ref.3, f32[32,1024]{1,0:T(8,128)} %means_ref.1, f32[32,1024]{1,0:T(8,128)} %var_ref.1, f32[32,1]{1,0:T(8,128)} %copy.9.logw_ref), custom_call_target="tpu_custom_call" | custom-call | tf_op jit(solution)/shard_map/scores/pallas_call | solution.py:467
  86.9 0.0 copy-start
  87.0 0.0 copy-start.1
  87.0 73.1 %moments.1 = (f32[32,1024]{1,0:T(8,128)}, f32[32,1152]{1,0:T(8,128)}) custom-call(f32[1024,1024]{1,0:T(8,128)} %x_ref.3, f32[1024,1024]{1,0:T(8,128)} %get-tuple-element.8.scores_ref, f32[8,1024]{1,0:T(8,128)} %get-tuple-element.9.norm_ref), custom_call_target="tpu_custom_call" | custom-call | tf_op jit(solution)/shard_map/moments/pallas_call | solution.py:488
  160.0 1.4 slice.11
  161.4 1.3 multiply_reduce_fusion
  162.7 0.0 copy-done
  162.7 0.0 copy-done.1
  162.7 1.8 %multiply_subtract_fusion = (f32[32,1024]{1,0:T(8,128)}, f32[32,1024]{1,0:T(8,128)}) fusion(f32[32,1024]{1,0:T(8,128)S(1)} %copy-done, f32[32,1024]{1,0:T(8,128)S(1)} %copy-done.1, f32[32,1152]{1,0:T(8,128)} %get-tuple-element.11, f32[32]{0:T(128)S(1)} %get-tuple-element.13, f32[32,1024]{1,0:T(8,128)} %get-tuple-element.10), kind=kLoop, calls=%fused_computation | loop fusion | flops 262144 | bytes 786560 | tf_op jit(solution)/shard_map/sub | solution.py:511
Async XLA Ops:
  86.9 75.8 %copy-start = (f32[32,1024]{1,0:T(8,128)S(1)}, f32[32,1024]{1,0:T(8,128)}, u32[]{:S(2)}) copy-start(f32[32,1024]{1,0:T(8,128)} %means_ref.1) | copy-start | bytes 393220
  87.0 75.8 %copy-start.1 = (f32[32,1024]{1,0:T(8,128)S(1)}, f32[32,1024]{1,0:T(8,128)}, u32[]{:S(2)}) copy-start(f32[32,1024]{1,0:T(8,128)} %var_ref.1) | copy-start | bytes 393220

commit v2 on v0

v2 whole, which is shorter than its diff:
```python
import functools

import jax
import jax.numpy as jnp
from jax import lax
from jax.experimental import pallas as pl
from jax.experimental.pallas import tpu as pltpu
from jax.sharding import PartitionSpec as P

circle_log = 1.8378770664093453
MESH = pl.DeviceIdType.MESH
NX = 4
LAG = 1.6
UNIT = 2.8
PAD = 128
IN_STREAMS = ((0, 0.0, 1.0, False), (1, 0.0, 2.0, False))
OUT_STREAMS = ((0, 0.0, 1.0, False), (1, 0.0, 2.0, False))


def columns(stream, width):
    _, lo, hi, _ = stream
    return int(lo * width), width + PAD if hi > 1.0 else int(hi * width)


def weight(stream):
    lo, hi = columns(stream, 1024)
    return (hi - lo) / 1024 * UNIT


def sign(v):
    return (v > 0) - (v < 0)


def canon(d, n):
    d = d % n
    return d if d <= n // 2 else d - n


def hops_on(d, n):
    out = []
    for way in (1, -1):
        if d != 0 and (d > 0) == (way > 0):
            continue
        if abs(d) == n // 2:
            continue
        new = d - way
        if abs(new) < n // 2:
            out.append((way, new, None))
        elif abs(new) == n // 2:
            out.append((way, n // 2, 0 if way > 0 else 1))
    return out


def axes_of(stream):
    return ("x", "z") if stream[3] else ("z", "x")


def gather_sends(stream, df, ds, nf, ns):
    first, second = axes_of(stream)
    out = []
    if ds == 0:
        out += [(first, way, (d, 0, half)) for way, d, half in hops_on(df, nf)]
    out += [(second, way, (df, d, half)) for way, d, half in hops_on(ds, ns)]
    return out


def gather_plan(nx, nz, ny):
    size = {"x": nx, "z": nz}
    free, arrivals, plan = {}, [], []
    t = 0.0
    halves = {}
    left = {(b, dx): nz * sum(s[0] == b for s in IN_STREAMS) for b in (0, 1) for dx in range(nx)}
    rows_left = 4 * ny
    whole, dots = [], []

    def push(axis, way, work, event):
        start = max(t, free.get((axis, way), 0.0))
        free[(axis, way)] = start + work
        arrivals.append((start + work + LAG, str(event), event))

    def available(k, df, ds):
        stream = IN_STREAMS[k]
        first, second = axes_of(stream)
        for axis, way, slot in gather_sends(stream, df, ds, size[first], size[second]):
            work = weight(stream) * (0.5 if slot[2] is not None else 1.0) * (2 if axis == "z" else 1)
            push(axis, way, work, ("recv", k, slot))
            plan.append(("send", k, (df, ds), axis, way, slot))
        dx = (df if stream[3] else ds) % nx
        left[(stream[0], dx)] -= 1
        if left[(stream[0], dx)] == 0:
            whole.append((stream[0], dx))
            dots.append((stream[0], dx, 0))
            if rows_left == 0:
                dots.append((stream[0], dx, 1))

    def rows_on(dy, q):
        for way, new, half in hops_on(dy, ny):
            if half is None or half == q:
                push("y", way, 2 * UNIT, ("rows", "y", new, q))
                plan.append(("rows_send", "y", way, dy, new, q))
        push("c", 1, UNIT / 3, ("rows", "c", dy, q))
        plan.append(("rows_send", "c", 0, dy, dy, q))

    for k in range(len(IN_STREAMS)):
        available(k, 0, 0)
    for q in (0, 1):
        push("z", 1, 2 * UNIT, ("rows", "p", 0, q))
        plan.append(("rows_send", "p", 0, 0, 0, q))
    plan.append(("split",))
    t += 2.5
    while arrivals or dots:
        arrivals.sort(key=lambda a: a[:2])
        if arrivals and arrivals[0][0] <= t or not dots:
            when, _, event = arrivals.pop(0)
            t = max(t, when)
            plan.append(event)
            if event[0] == "rows":
                if event[1] != "c":
                    rows_on(*event[2:])
                plan.append(("rows_split",) + event[1:])
                t += 0.2
                rows_left -= 1
                if rows_left == 0:
                    dots += [w + (1,) for w in whole]
                continue
            _, k, (df, ds, half) = event
            if half is not None:
                halves[(k, df, ds)] = halves.get((k, df, ds), 0) + 1
                if halves[(k, df, ds)] < 2:
                    continue
            available(k, df, ds)
        else:
            plan.append(("dot",) + dots.pop(0))
            t += 1.4
    return plan


def reduce_inputs(stream, df, ds, nf, ns):
    def along(d, n):
        if d == 0:
            return [(1, None), (-1, None)] if n > 2 else [(1, 0), (1, 1)]
        if abs(d) == n // 2:
            return []
        far = d + sign(d)
        if abs(far) == n // 2:
            return [(n // 2, 0 if d > 0 else 1)]
        return [(far, None)]

    out = [(df, d, half) for d, half in along(ds, ns)]
    if ds == 0:
        out += [(d, 0, half) for d, half in along(df, nf)]
    return out


def reduce_sends(stream, df, ds, nf, ns):
    first, second = axes_of(stream)
    axis, d, n = (second, ds, ns) if ds != 0 else (first, df, nf)
    if d == 0:
        return []
    if abs(d) == n // 2:
        return [(axis, 1, (df, ds, 0)), (axis, -1, (df, ds, 1))]
    return [(axis, sign(d), (df, ds, None))]


def reduce_plan(nx, nz):
    size = {"x": nx, "z": nz}
    free, arrivals, plan = {}, [], []
    t = 0.0
    groups = sorted(range(nx), key=lambda dx: (-abs(canon(dx, nx)), dx))
    done, landed = set(), set()
    waiting = []
    for k, stream in enumerate(OUT_STREAMS):
        first, second = axes_of(stream)
        for f in range(size[first]):
            for s in range(size[second]):
                waiting.append((k, canon(f, size[first]), canon(s, size[second])))

    def is_ready(item):
        k, df, ds = item
        stream = OUT_STREAMS[k]
        first, second = axes_of(stream)
        if (df if stream[3] else ds) % nx not in done:
            return False
        needs = reduce_inputs(stream, df, ds, size[first], size[second])
        return all((k, n) in landed for n in needs)

    while waiting:
        for a in [a for a in arrivals if a[0] <= t]:
            arrivals.remove(a)
            landed.add(a[1:])
        ready = sorted((w for w in waiting if is_ready(w)), key=lambda w: (-abs(w[1]) - abs(w[2]), w))
        if ready:
            item = ready[0]
            waiting.remove(item)
            k, df, ds = item
            stream = OUT_STREAMS[k]
            first, second = axes_of(stream)
            plan.append(("sum", k, (df, ds)))
            t += 0.15
            for axis, way, slot in reduce_sends(stream, df, ds, size[first], size[second]):
                work = weight(stream) * (0.5 if slot[2] is not None else 1.0) * (2 if axis == "z" else 1)
                start = max(t, free.get((axis, way), 0.0))
                free[(axis, way)] = start + work
                arrivals.append((start + work + LAG, k, slot))
        elif groups:
            dx = groups.pop(0)
            plan.append(("moments", dx))
            t += 4.5
            done.add(dx)
        else:
            t = min(a[0] for a in arrivals)
    return plan


class Place:
    def __init__(self, nx, nz, comps):
        self.nx, self.nz, self.ny = nx, nz // 2, comps // 2
        me = lax.axis_index("dp")
        self.x, z = me // nz, me % nz
        self.j, self.parity = z // 2, z % 2
        self.comp = lax.axis_index("comp")
        self.y, self.core = self.comp // 2, self.comp % 2
        self.full_z = nz

    def block(self, dx, dz):
        return ((self.x + dx) % self.nx) * self.nz + (self.j + dz) % self.nz

    def of(self, stream, df, ds):
        return self.block(df, ds) if stream[3] else self.block(ds, df)

    def group(self, dx):
        return (self.x + dx) % self.nx

    def neighbour(self, axis, way):
        x, j = (self.x + way, self.j) if axis == "x" else (self.x, self.j + way)
        return {"dp": (x % self.nx) * self.full_z + 2 * (j % self.nz) + self.parity}

    def partner(self):
        return {"dp": self.x * self.full_z + 2 * self.j + 1 - self.parity}

    def row_target(self, kind, way):
        if kind == "p":
            return self.partner()
        if kind == "y":
            return {"comp": ((self.y + way) % self.ny) * 2 + self.core}
        return {"comp": self.y * 2 + 1 - self.core}

    def slot(self, k, stream, slot):
        df, ds, half = slot
        nf, ns = (self.nx, self.nz) if stream[3] else (self.nz, self.nx)
        return ((k * nf + df % nf) * ns + ds % ns) * 2 + (half or 0)


def part(ref, index, half, cols):
    rows = ref.shape[1]
    at = pl.ds(0, rows) if half is None else pl.ds(half * (rows // 2), rows // 2)
    return ref.at[index, at, pl.ds(cols[0], cols[1] - cols[0])]


def split(x):
    high = x.astype(jnp.bfloat16)
    return high, (x - high.astype(jnp.float32)).astype(jnp.bfloat16)


def dot_nt(a, b):
    return lax.dot_general(a, b, (((1,), (1,)), ((), ())), preferred_element_type=jnp.float32)


def dot_nn(a, b):
    return jnp.dot(a, b, preferred_element_type=jnp.float32)


def kernel(
    nx, nz, comps, x_ref, means_ref, var_ref, logw_ref, first_ref, second_ref, loglik_ref,
    scaled, prec, other, xh, xl, qh, ql, ph, plo, scores, stat, norm, rh, rl,
    sum_a, sum_b, land_a, land_b,
    in_send, in_recv, out_send, out_recv, row_send, row_recv, stat_send, stat_recv,
):
    place = Place(nx, nz, comps)
    nz, ny = place.nz, place.ny
    rows, width = x_ref.shape
    size = means_ref.shape[0]
    group = nz * size
    own = place.block(0, 0)
    parity, comp = place.parity, place.comp
    own_rows = pl.multiple_of(parity * rows, rows)
    other_rows = pl.multiple_of((1 - parity) * rows, rows)
    sub = rows // comps // 2
    variances = var_ref[...]
    means = means_ref[...]
    p = 1.0 / variances
    sc = means * p
    offset = (
        logw_ref[...]
        - 0.5 * jnp.sum(jnp.log(variances), axis=1, keepdims=True)
        - 0.5 * jnp.sum(means * sc, axis=1, keepdims=True)
    )
    scaled[own] = sc
    prec[own, :, 0:width] = -0.5 * (p - 1.0)
    prec[own, :, width : width + PAD] = jnp.broadcast_to(offset, (size, PAD))

    barrier = pltpu.get_barrier_semaphore()
    friends = [place.neighbour(axis, way) for axis in ("x", "z") for way in (1, -1)]
    friends += [{"comp": (comp + k) % comps} for k in range(1, comps)]
    friends += [dict(place.partner(), comp=(comp + k) % comps) for k in range(comps)]
    for friend in friends:
        pl.semaphore_signal(barrier, inc=1, device_id=friend, device_id_type=MESH)
    pl.semaphore_wait(barrier, len(friends))

    started = []

    def begin(c):
        c.start()
        started.append(c)

    def remote(src, dst, send, recv, target):
        return pltpu.make_async_remote_copy(
            src_ref=src, dst_ref=dst, send_sem=send, recv_sem=recv, device_id=target, device_id_type=MESH
        )

    bufs = (scaled, prec)

    def param_copy(k, offs, axis, way, slot):
        stream = IN_STREAMS[k]
        n = place.slot(k, stream, slot)
        ref = part(bufs[stream[0]], place.of(stream, *offs), slot[2], columns(stream, width))
        return remote(ref, ref, in_send.at[n], in_recv.at[n], place.neighbour(axis, way))

    def slice_of(kind, dy, q):
        core = 1 - place.core if kind == "c" else place.core
        return (((place.y + dy) % ny) * 2 + core) * 2 + q

    def row_sem(kind, new, q):
        return ((("p", "y", "c").index(kind)) * ny + new % ny) * 2 + q

    def row_copy(kind, way, dy, new, q):
        index = slice_of("p", dy, q)
        n = row_sem(kind, new, q)
        if kind == "p":
            src = x_ref.at[pl.ds(pl.multiple_of(index * sub, sub), sub), :]
        else:
            src = other.at[index]
        return remote(src, other.at[index], row_send.at[n], row_recv.at[n], place.row_target(kind, way))

    def split_into(base, x):
        at = pl.ds(base, x.shape[0])
        xh[at, :], xl[at, :] = split(x)
        qh[at, :], ql[at, :] = split(x * x)

    tile = min(256, rows)
    begun = set()
    formed = set()
    for op in gather_plan(nx, nz, ny):
        if op[0] == "send":
            begin(param_copy(*op[1:]))
        elif op[0] == "recv":
            _, k, slot = op
            param_copy(k, slot[:2], "x", 1, slot).wait_recv()
        elif op[0] == "rows_send":
            begin(row_copy(*op[1:]))
        elif op[0] == "rows":
            _, kind, dy, q = op
            ref = other.at[slice_of(kind, dy, q)]
            n = row_sem(kind, dy, q)
            remote(ref, ref, row_send.at[n], row_recv.at[n], place.partner()).wait_recv()
        elif op[0] == "rows_split":
            _, kind, dy, q = op
            index = slice_of(kind, dy, q)
            split_into(pl.multiple_of(other_rows + index * sub, sub), other[index])
        elif op[0] == "split":
            few = min(64, rows)

            @pl.loop(0, rows // few)
            def _(i):
                at = pl.multiple_of(i * few, few)
                split_into(pl.multiple_of(own_rows + at, few), x_ref[pl.ds(at, few), :])
        else:
            _, b, dx, h = op
            g = place.group(dx)
            blocks = pl.ds(pl.multiple_of(g * nz, nz), nz)
            at = pl.ds(pl.multiple_of(g * group, group), group)
            ph[...], plo[...] = split(bufs[b][blocks, :, 0:width].reshape(group, width))
            high, low = (xh, xl) if b == 0 else (qh, ql)
            last = (dx, h) in formed
            formed.add((dx, h))
            opening = last and h not in begun
            if last:
                begun.add(h)
            base = own_rows if h == 0 else other_rows

            @pl.loop(0, rows // tile)
            def _(i):
                n = pl.ds(pl.multiple_of(base + i * tile, tile), tile)
                s = dot_nt(ph[...], high[n, :]) + dot_nt(ph[...], low[n, :]) + dot_nt(plo[...], high[n, :])
                if not last:
                    scores[at, n] = s
                    return
                off = prec[blocks, :, width : width + PAD].reshape(group, PAD)[:, 0:1]
                s = s + scores[at, n] + off
                scores[at, n] = s
                peak = jnp.max(s, axis=0, keepdims=True)
                if opening:
                    norm[0:1, n] = peak
                    norm[1:2, n] = jnp.sum(jnp.exp(s - peak), axis=0, keepdims=True)
                else:
                    before = norm[0:1, n]
                    now = jnp.maximum(before, peak)
                    norm[1:2, n] = norm[1:2, n] * jnp.exp(before - now) + jnp.sum(
                        jnp.exp(s - now), axis=0, keepdims=True
                    )
                    norm[0:1, n] = now

    mine = parity * comps + comp
    stat[mine] = norm[0:2, :]
    peers = [(0, k) for k in range(1, comps)] + [(1, k) for k in range(comps)]
    for other_z, k in peers:
        target = {"comp": (comp + k) % comps}
        if other_z:
            target.update(place.partner())
        n = other_z * comps + k
        begin(remote(stat.at[mine], stat.at[mine], stat_send.at[n], stat_recv.at[n], target))
    ones = jnp.ones((8, width), jnp.bfloat16)

    @pl.loop(0, rows // tile)
    def _(i):
        n = pl.ds(pl.multiple_of(own_rows + i * tile, tile), tile)
        here = pl.ds(pl.multiple_of(i * tile, tile), tile)
        loglik_ref[:, here] = 0.5 * (dot_nt(ones, qh[n, :]) + dot_nt(ones, ql[n, :])) + 0.5 * width * circle_log

    for other_z, k in peers:
        source = ((1 - parity) if other_z else parity) * comps + (comp - k + comps) % comps
        n = other_z * comps + k
        ref = stat.at[source]
        remote(ref, ref, stat_send.at[n], stat_recv.at[n], place.partner()).wait_recv()
    peak = stat[0, 0:1, :]
    for c in range(1, 2 * comps):
        peak = jnp.maximum(peak, stat[c, 0:1, :])
    total = jnp.zeros_like(peak)
    for c in range(2 * comps):
        total = total + stat[c, 1:2, :] * jnp.exp(stat[c, 0:1, :] - peak)
    norm[0:1, :] = peak + jnp.log(total)
    loglik_ref[0:1, :] = norm[0:1, pl.ds(own_rows, rows)] - loglik_ref[0:1, :]

    sums, lands, results = (sum_a, sum_b), (land_a, land_b), (first_ref, second_ref)

    def sum_copy(k, axis, way, slot):
        stream = OUT_STREAMS[k]
        df, ds, half = slot
        b, cols = stream[0], columns(stream, width)
        n = place.slot(k, stream, slot)
        return remote(
            part(sums[b], place.of(stream, df, ds), half, cols),
            part(lands[b], landing(k, slot), half, cols),
            out_send.at[n],
            out_recv.at[n],
            place.neighbour(axis, way),
        )

    def landing(k, slot):
        return place.slot(0, OUT_STREAMS[k], slot) // 2

    for op in reduce_plan(nx, nz):
        if op[0] == "moments":
            g = place.group(op[1])
            base = g * nz

            @pl.loop(0, nz)
            def _(i):
                at = pl.ds(pl.multiple_of(g * group + i * size, size), size)
                here = pl.ds(pl.multiple_of(i * size, size), size)
                r = jnp.exp(scores[at, :] - norm[0:1, :])
                rh[here, :], rl[here, :] = split(r)
                counts = jnp.sum(r, axis=1, keepdims=True)
                sum_b[base + i, :, width : width + PAD] = jnp.broadcast_to(counts, (size, PAD))

            blocks = pl.ds(pl.multiple_of(base, nz), nz)
            cols = min(256, width)

            @pl.loop(0, width // cols)
            def _(i):
                d = pl.ds(pl.multiple_of(i * cols, cols), cols)
                a = dot_nn(rh[...], xh[:, d]) + dot_nn(rh[...], xl[:, d]) + dot_nn(rl[...], xh[:, d])
                sum_a[blocks, :, d] = a.reshape(nz, size, cols)
                b = dot_nn(rh[...], qh[:, d]) + dot_nn(rh[...], ql[:, d]) + dot_nn(rl[...], qh[:, d])
                sum_b[blocks, :, d] = b.reshape(nz, size, cols)
            continue
        _, k, (df, ds) = op
        stream = OUT_STREAMS[k]
        nf, ns = (nx, nz) if stream[3] else (nz, nx)
        index = place.of(stream, df, ds)
        whole, cut = [], []
        for slot in reduce_inputs(stream, df, ds, nf, ns):
            sum_copy(k, "x", 1, slot).wait_recv()
            (whole if slot[2] is None else cut).append(slot)
        lo, hi = columns(stream, width)
        out, land = sums[stream[0]], lands[stream[0]]
        if whole:
            v = out[index, :, lo:hi]
            for slot in whole:
                v = v + land[landing(k, slot), :, lo:hi]
            out[index, :, lo:hi] = v
        for slot in cut:
            at = pl.ds(slot[2] * (size // 2), size // 2)
            out[index, at, lo:hi] = out[index, at, lo:hi] + land[landing(k, slot), at, lo:hi]
        if (df, ds) == (0, 0):
            results[stream[0]][:, lo:hi] = out[index, :, lo:hi]
        for axis, way, slot in reduce_sends(stream, df, ds, nf, ns):
            begin(sum_copy(k, axis, way, slot))
    for c in started:
        c.wait_send()


def per_device(nx, nz, comps, x, means, variances, log_weights):
    rows, width = x.shape
    size = means.shape[0]
    count = nx * nz // 2
    group = nz // 2 * size
    vmem = pl.BlockSpec(memory_space=pltpu.VMEM)
    f32, bf16 = jnp.float32, jnp.bfloat16
    dma = pltpu.SemaphoreType.DMA
    first, second, loglik = pl.pallas_call(
        functools.partial(kernel, nx, nz, comps),
        out_shape=(
            jax.ShapeDtypeStruct((size, width), f32),
            jax.ShapeDtypeStruct((size, width + PAD), f32),
            jax.ShapeDtypeStruct((8, rows), f32),
        ),
        in_specs=[vmem] * 4,
        out_specs=(vmem, vmem, vmem),
        scratch_shapes=[
            pltpu.VMEM((count, size, width), f32),
            pltpu.VMEM((count, size, width + PAD), f32),
            pltpu.VMEM((2 * comps, rows // comps // 2, width), f32),
            *[pltpu.VMEM((2 * rows, width), bf16)] * 4,
            *[pltpu.VMEM((group, width), bf16)] * 2,
            pltpu.VMEM((count * size, 2 * rows), f32),
            pltpu.VMEM((2 * comps, 2, 2 * rows), f32),
            pltpu.VMEM((8, 2 * rows), f32),
            *[pltpu.VMEM((group, 2 * rows), bf16)] * 2,
            *[pltpu.VMEM((count, size, width), f32), pltpu.VMEM((count, size, width + PAD), f32)] * 2,
            *[dma((2 * count * len(IN_STREAMS),))] * 2,
            *[dma((2 * count * len(OUT_STREAMS),))] * 2,
            *[dma((3 * comps,))] * 2,
            *[dma((2 * comps,))] * 2,
        ],
        compiler_params=pltpu.CompilerParams(
            collective_id=0, has_side_effects=True, vmem_limit_bytes=60 << 20
        ),
        name="mixture",
    )(x, means, variances, log_weights[:, None])
    counts = second[:, width]
    denom = (counts + 1.0)[:, None]
    new_means = (first + means) / denom
    new_variances = (second[:, :width] + variances + means * means) / denom - new_means * new_means
    new_weights = counts / (rows * nx * nz)
    return (new_means, new_variances, new_weights, loglik[0])


def solution(mesh):
    count, comps = mesh.shape["dp"], mesh.shape["comp"]
    return jax.shard_map(
        functools.partial(per_device, NX, count // NX, comps),
        mesh=mesh,
        in_specs=(
            P("dp", None),
            P(("comp", "dp"), None),
            P(("comp", "dp"), None),
            P(("comp", "dp")),
        ),
        out_specs=(P(("comp", "dp"), None), P(("comp", "dp"), None), P(("comp", "dp")), P("dp")),
        check_vma=False,
    )
```

time: 526 us -> 156 us (0.30); the launches traced: 517 us -> 156 us
  waiting for transfers between devices: 238 us -> 0 us
  blocking collectives: 173 us -> 0 us
  Pallas kernels: 0 us -> 149 us
  matrix products: 60.3 us -> 0 us
  between operations: 15.7 us -> 0.66 us
  other arithmetic: 17.2 us -> 3.11 us
  local copies, waits for them, and re-layouts: 12.1 us -> 2.75 us
    unnamed x2 -> x0, blocking collectives: 151 us -> none
    reduce_scatter x1 -> x0, waiting for transfers between devices: 149 us -> none  [per_device(): lax.psum_scatter(jnp.concatenate([weighted_sum(resp, embeddings), weighte...]
    pallas_call x0 -> x1, Pallas kernels: none -> 149 us  [per_device(): pl.pallas_call(functools.partial(kernel, nx, nz, comps), out_shape=(jax.S...]
    all_gather x2 -> x0, waiting for transfers between devices: 87.3 us -> none  [the longest x1 81.7 us: per_device(): lax.all_gather(variances, 'dp', axis=0, tiled=True)]
    dot_general x4 -> x0, matrix products: 60.3 us -> none  [the longest x2 31.5 us: weighted_sum(): lax.dot_general(resp, values, (((0,), (0,)), ((), ())), precision=lax.Pre...]
    psum x1 -> x0, blocking collectives: 12.4 us -> none  [per_device(): total = lax.psum(jnp.sum(jnp.exp(scores - peak[:, None]), axis=1), 'comp')]
    unnamed x20 -> x4, local copies, waits for them, and re-layouts: 12.1 us -> 0.01 us
    reduce_sum x3 -> x0, other arithmetic: 10.8 us -> none  [the longest x1 5.15 us: component_terms(): jnp.sum(jnp.log(variances), axis=1)]
  transfers between devices with their start and end apart: 3 -> 0, of which waited for: 3 -> 0; matrix products, arithmetic and copies ran while one was open for 1% -> 0% of each run, Pallas kernels for 0% -> 0%
where the time goes in v2:
time: 156 us
  Pallas kernels  149 us (96%)
  other arithmetic  3.11 us (2%)
  local copies, waits for them, and re-layouts  2.75 us (2%)
    pallas_call x1, Pallas kernels, per_device(): pl.pallas_call(functools.partial(kernel, nx, nz, comps), out_shape=(jax.S...  149 us

profile of v2, /device:TPU:8, one launch (start us, length us, event | category | flops | bytes accessed | tf_op | source)
XLA Modules:
  0.0 155.7 jit_solution(11985035332859632213)
XLA Ops:
  0.6 0.0 copy-start.1
  0.6 0.0 copy-start
  0.7 1.4 copy.9.logw_ref
  2.0 149.2 %mixture.1 = (f32[32,1024]{1,0:T(8,128)}, f32[32,1152]{1,0:T(8,128)}, f32[8,1024]{1,0:T(8,128)}) custom-call(f32[1024,1024]{1,0:T(8,128)} %x_ref.1, f32[32,1024]{1,0:T(8,128)} %means_ref.1, f32[32,1024]{1,0:T(8,128)} %var_ref.1, f32[32,1]{1,0:T(8,128)} %copy.9.logw_ref), custom_call_target="tpu_custom_call" | custom-call | tf_op jit(solution)/shard_map/mixture/pallas_call | solution.py:521
  151.3 1.3 multiply_reduce_fusion
  152.6 0.0 copy-done.1
  152.6 0.0 copy-done
  152.6 1.8 %multiply_subtract_fusion = (f32[32,1024]{1,0:T(8,128)}, f32[32,1024]{1,0:T(8,128)}) fusion(f32[32,1024]{1,0:T(8,128)S(1)} %copy-done, f32[32,1024]{1,0:T(8,128)S(1)} %copy-done.1, f32[32,1152]{1,0:T(8,128)} %get-tuple-element.8, f32[32]{0:T(128)S(1)} %get-tuple-element.11, f32[32,1024]{1,0:T(8,128)} %get-tuple-element.7), kind=kLoop, calls=%fused_computation | loop fusion | flops 262144 | bytes 786560 | tf_op jit(solution)/shard_map/sub | solution.py:554
  154.4 1.4 slice.11
Async XLA Ops:
  0.6 152.0 %copy-start.1 = (f32[32,1024]{1,0:T(8,128)S(1)}, f32[32,1024]{1,0:T(8,128)}, u32[]{:S(2)}) copy-start(f32[32,1024]{1,0:T(8,128)} %var_ref.1) | copy-start | bytes 393220
  0.6 152.0 %copy-start = (f32[32,1024]{1,0:T(8,128)S(1)}, f32[32,1024]{1,0:T(8,128)}, u32[]{:S(2)}) copy-start(f32[32,1024]{1,0:T(8,128)} %means_ref.1) | copy-start | bytes 393220

commit v3 on v2

--- a/solution.py
+++ b/solution.py
@@ -271,15 +271,17 @@
 
 
 def kernel(
-    nx, nz, comps, x_ref, means_ref, var_ref, logw_ref, first_ref, second_ref, loglik_ref,
-    scaled, prec, other, xh, xl, qh, ql, ph, plo, scores, stat, norm, rh, rl,
+    nx, nz, comps, x_hbm, means_ref, var_ref, logw_ref, first_ref, second_ref, loglik_ref,
+    scaled, prec, other, x_ref, xh, xl, qh, ql, pt, scores, stat, norm, rh, rl,
     sum_a, sum_b, land_a, land_b,
-    in_send, in_recv, out_send, out_recv, row_send, row_recv, stat_send, stat_recv,
+    in_send, in_recv, out_send, out_recv, row_send, row_recv, stat_send, stat_recv, load_sem,
 ):
     place = Place(nx, nz, comps)
     nz, ny = place.nz, place.ny
     rows, width = x_ref.shape
     size = means_ref.shape[0]
+    load = pltpu.make_async_copy(x_hbm, x_ref, load_sem)
+    load.start()
     group = nz * size
     own = place.block(0, 0)
     parity, comp = place.parity, place.comp
@@ -290,8 +292,9 @@
     means = means_ref[...]
     p = 1.0 / variances
     sc = means * p
+    diagonal = lax.broadcasted_iota(jnp.int32, (size, size), 0) == lax.broadcasted_iota(jnp.int32, (size, size), 1)
     offset = (
-        logw_ref[...]
+        jnp.sum(jnp.where(diagonal, logw_ref[...], 0.0), axis=1, keepdims=True)
         - 0.5 * jnp.sum(jnp.log(variances), axis=1, keepdims=True)
         - 0.5 * jnp.sum(means * sc, axis=1, keepdims=True)
     )
@@ -306,6 +309,7 @@
     for friend in friends:
         pl.semaphore_signal(barrier, inc=1, device_id=friend, device_id_type=MESH)
     pl.semaphore_wait(barrier, len(friends))
+    load.wait()
 
     started = []
 
@@ -347,7 +351,8 @@
         xh[at, :], xl[at, :] = split(x)
         qh[at, :], ql[at, :] = split(x * x)
 
-    tile = min(256, rows)
+    tile = min(512, rows)
+    ones = jnp.ones((8, width), jnp.bfloat16)
     begun = set()
     formed = set()
     for op in gather_plan(nx, nz, ny):
@@ -374,12 +379,22 @@
             def _(i):
                 at = pl.multiple_of(i * few, few)
                 split_into(pl.multiple_of(own_rows + at, few), x_ref[pl.ds(at, few), :])
+
+            few = min(256, rows)
+
+            @pl.loop(0, rows // few)
+            def _(i):
+                n = pl.ds(pl.multiple_of(own_rows + i * few, few), few)
+                here = pl.ds(pl.multiple_of(i * few, few), few)
+                square = dot_nt(ones, qh[n, :]) + dot_nt(ones, ql[n, :])
+                loglik_ref[:, here] = 0.5 * square + 0.5 * width * circle_log
         else:
             _, b, dx, h = op
             g = place.group(dx)
             blocks = pl.ds(pl.multiple_of(g * nz, nz), nz)
             at = pl.ds(pl.multiple_of(g * group, group), group)
-            ph[...], plo[...] = split(bufs[b][blocks, :, 0:width].reshape(group, width))
+            turned = bufs[b][blocks, :, 0:width].reshape(group, width).T
+            pt[:, 0:group], pt[:, group : 2 * group] = split(turned)
             high, low = (xh, xl) if b == 0 else (qh, ql)
             last = (dx, h) in formed
             formed.add((dx, h))
@@ -391,7 +406,9 @@
             @pl.loop(0, rows // tile)
             def _(i):
                 n = pl.ds(pl.multiple_of(base + i * tile, tile), tile)
-                s = dot_nt(ph[...], high[n, :]) + dot_nt(ph[...], low[n, :]) + dot_nt(plo[...], high[n, :])
+                both = dot_nn(high[n, :], pt[...])
+                s = both[:, 0:group] + both[:, group : 2 * group] + dot_nn(low[n, :], pt[:, 0:group])
+                s = s.T
                 if not last:
                     scores[at, n] = s
                     return
@@ -419,13 +436,6 @@
             target.update(place.partner())
         n = other_z * comps + k
         begin(remote(stat.at[mine], stat.at[mine], stat_send.at[n], stat_recv.at[n], target))
-    ones = jnp.ones((8, width), jnp.bfloat16)
-
-    @pl.loop(0, rows // tile)
-    def _(i):
-        n = pl.ds(pl.multiple_of(own_rows + i * tile, tile), tile)
-        here = pl.ds(pl.multiple_of(i * tile, tile), tile)
-        loglik_ref[:, here] = 0.5 * (dot_nt(ones, qh[n, :]) + dot_nt(ones, ql[n, :])) + 0.5 * width * circle_log
 
     for other_z, k in peers:
         source = ((1 - parity) if other_z else parity) * comps + (comp - k + comps) % comps
@@ -525,14 +535,15 @@
             jax.ShapeDtypeStruct((size, width + PAD), f32),
             jax.ShapeDtypeStruct((8, rows), f32),
         ),
-        in_specs=[vmem] * 4,
+        in_specs=[pl.BlockSpec(memory_space=pl.ANY)] + [vmem] * 3,
         out_specs=(vmem, vmem, vmem),
         scratch_shapes=[
             pltpu.VMEM((count, size, width), f32),
             pltpu.VMEM((count, size, width + PAD), f32),
             pltpu.VMEM((2 * comps, rows // comps // 2, width), f32),
+            pltpu.VMEM((rows, width), f32),
             *[pltpu.VMEM((2 * rows, width), bf16)] * 4,
-            *[pltpu.VMEM((group, width), bf16)] * 2,
+            pltpu.VMEM((width, 2 * group), bf16),
             pltpu.VMEM((count * size, 2 * rows), f32),
             pltpu.VMEM((2 * comps, 2, 2 * rows), f32),
             pltpu.VMEM((8, 2 * rows), f32),
@@ -542,12 +553,13 @@
             *[dma((2 * count * len(OUT_STREAMS),))] * 2,
             *[dma((3 * comps,))] * 2,
             *[dma((2 * comps,))] * 2,
+            dma,
         ],
         compiler_params=pltpu.CompilerParams(
             collective_id=0, has_side_effects=True, vmem_limit_bytes=60 << 20
         ),
         name="mixture",
-    )(x, means, variances, log_weights[:, None])
+    )(x, means, variances, log_weights[None, :])
     counts = second[:, width]
     denom = (counts + 1.0)[:, None]
     new_means = (first + means) / denom

time: 156 us -> 140 us (0.90)
  Pallas kernels: 149 us -> 135 us
    pallas_call x1, Pallas kernels: 149 us -> 135 us  [per_device(): pl.pallas_call(functools.partial(kernel, nx, nz, comps), out_shape=(jax.S...]
where the time goes in v3:
time: 140 us
  Pallas kernels  135 us (96%)
  other arithmetic  3.11 us (2%)
    pallas_call x1, Pallas kernels, per_device(): pl.pallas_call(functools.partial(kernel, nx, nz, comps), out_shape=(jax.S...  135 us

profile of v3, /device:TPU:8, one launch (start us, length us, event | category | flops | bytes accessed | tf_op | source)
XLA Modules:
  0.0 139.9 jit_solution(16696340395215581158)
XLA Ops:
  0.6 0.0 copy-start.1
  0.6 0.0 copy-start
  0.7 134.8 %mixture.1 = (f32[32,1024]{1,0:T(8,128)}, f32[32,1152]{1,0:T(8,128)}, f32[8,1024]{1,0:T(8,128)}) custom-call(f32[1024,1024]{1,0:T(8,128)} %x_hbm.1, f32[32,1024]{1,0:T(8,128)} %means_ref.1, f32[32,1024]{1,0:T(8,128)} %var_ref.1, f32[1,32]{1,0:T(1,128)} %bitcast.3), custom_call_target="tpu_custom_call" | custom-call | tf_op jit(solution)/shard_map/mixture/pallas_call | solution.py:531
  135.4 1.3 multiply_reduce_fusion
  136.8 0.0 copy-done.1
  136.8 0.0 copy-done
  136.8 1.8 %multiply_subtract_fusion = (f32[32,1024]{1,0:T(8,128)}, f32[32,1024]{1,0:T(8,128)}) fusion(f32[32,1024]{1,0:T(8,128)S(1)} %copy-done, f32[32,1024]{1,0:T(8,128)S(1)} %copy-done.1, f32[32,1152]{1,0:T(8,128)} %get-tuple-element.8, f32[32]{0:T(128)S(1)} %get-tuple-element.11, f32[32,1024]{1,0:T(8,128)} %get-tuple-element.7), kind=kLoop, calls=%fused_computation | loop fusion | flops 262144 | bytes 786560 | tf_op jit(solution)/shard_map/sub | solution.py:566
  138.6 1.4 slice.11
Async XLA Ops:
  0.6 136.2 %copy-start.1 = (f32[32,1024]{1,0:T(8,128)S(1)}, f32[32,1024]{1,0:T(8,128)}, u32[]{:S(2)}) copy-start(f32[32,1024]{1,0:T(8,128)} %var_ref.1) | copy-start | bytes 393220
  0.6 136.2 %copy-start = (f32[32,1024]{1,0:T(8,128)S(1)}, f32[32,1024]{1,0:T(8,128)}, u32[]{:S(2)}) copy-start(f32[32,1024]{1,0:T(8,128)} %means_ref.1) | copy-start | bytes 393220

commit v4 on v3

--- a/solution.py
+++ b/solution.py
@@ -70,8 +70,8 @@
     t = 0.0
     halves = {}
     left = {(b, dx): nz * sum(s[0] == b for s in IN_STREAMS) for b in (0, 1) for dx in range(nx)}
-    rows_left = 4 * ny
-    whole, dots = [], []
+    rows_left = {canon(y, ny): 4 for y in range(ny)}
+    whole, dots, here = [], [], []
 
     def push(axis, way, work, event):
         start = max(t, free.get((axis, way), 0.0))
@@ -89,9 +89,8 @@
         left[(stream[0], dx)] -= 1
         if left[(stream[0], dx)] == 0:
             whole.append((stream[0], dx))
-            dots.append((stream[0], dx, 0))
-            if rows_left == 0:
-                dots.append((stream[0], dx, 1))
+            dots.append(("turn", stream[0], dx))
+            dots.extend(("dot", stream[0], dx, c) for c in here)
 
     def rows_on(dy, q):
         for way, new, half in hops_on(dy, ny):
@@ -101,13 +100,29 @@
         push("c", 1, UNIT / 3, ("rows", "c", dy, q))
         plan.append(("rows_send", "c", 0, dy, dy, q))
 
+    def rows_here(chunk):
+        here.append(chunk)
+        dots.extend(("dot",) + w + (chunk,) for w in whole)
+
+    def rows_go(q):
+        push("z", 1, 2 * UNIT, ("rows", "p", 0, q))
+        plan.append(("rows_send", "p", 0, 0, 0, q))
+
+    def rows_after(k, d):
+        relays.discard((k, d))
+        if not relays and rows_sent == []:
+            for q in (0, 1):
+                rows_go(q)
+                rows_sent.append(q)
+
+    rows_sent = []
+    relays = {(k, d) for k in range(len(IN_STREAMS)) for d in ((-1, 1) if nz > 2 else (0,))}
     for k in range(len(IN_STREAMS)):
         available(k, 0, 0)
-    for q in (0, 1):
-        push("z", 1, 2 * UNIT, ("rows", "p", 0, q))
-        plan.append(("rows_send", "p", 0, 0, 0, q))
+        rows_after(k, 0)
     plan.append(("split",))
-    t += 2.5
+    t += 4.0
+    rows_here(None)
     while arrivals or dots:
         arrivals.sort(key=lambda a: a[:2])
         if arrivals and arrivals[0][0] <= t or not dots:
@@ -119,9 +134,9 @@
                     rows_on(*event[2:])
                 plan.append(("rows_split",) + event[1:])
                 t += 0.2
-                rows_left -= 1
-                if rows_left == 0:
-                    dots += [w + (1,) for w in whole]
+                rows_left[event[2]] -= 1
+                if rows_left[event[2]] == 0:
+                    rows_here(event[2])
                 continue
             _, k, (df, ds, half) = event
             if half is not None:
@@ -129,9 +144,12 @@
                 if halves[(k, df, ds)] < 2:
                     continue
             available(k, df, ds)
+            if ds == 0:
+                rows_after(k, df)
         else:
-            plan.append(("dot",) + dots.pop(0))
-            t += 1.4
+            op = dots.pop(0)
+            plan.append(op)
+            t += 0.3 if op[0] == "turn" else 1.6 if op[3] is None else 0.45
     return plan
 
 
@@ -351,7 +369,6 @@
         xh[at, :], xl[at, :] = split(x)
         qh[at, :], ql[at, :] = split(x * x)
 
-    tile = min(512, rows)
     ones = jnp.ones((8, width), jnp.bfloat16)
     begun = set()
     formed = set()
@@ -387,27 +404,34 @@
                 n = pl.ds(pl.multiple_of(own_rows + i * few, few), few)
                 here = pl.ds(pl.multiple_of(i * few, few), few)
                 square = dot_nt(ones, qh[n, :]) + dot_nt(ones, ql[n, :])
-                loglik_ref[:, here] = 0.5 * square + 0.5 * width * circle_log
+                loglik_ref[:, here] = 0.5 * square[0:1, :] + 0.5 * width * circle_log
+        elif op[0] == "turn":
+            _, b, dx = op
+            blocks = pl.ds(pl.multiple_of(place.group(dx) * nz, nz), nz)
+            turned = bufs[b][blocks, :, 0:width].reshape(group, width).T
+            pt[b * nx + dx, :, 0:group], pt[b * nx + dx, :, group : 2 * group] = split(turned)
         else:
             _, b, dx, h = op
             g = place.group(dx)
             blocks = pl.ds(pl.multiple_of(g * nz, nz), nz)
             at = pl.ds(pl.multiple_of(g * group, group), group)
-            turned = bufs[b][blocks, :, 0:width].reshape(group, width).T
-            pt[:, 0:group], pt[:, group : 2 * group] = split(turned)
+            params = pt.at[b * nx + dx]
             high, low = (xh, xl) if b == 0 else (qh, ql)
             last = (dx, h) in formed
             formed.add((dx, h))
             opening = last and h not in begun
             if last:
                 begun.add(h)
-            base = own_rows if h == 0 else other_rows
-
-            @pl.loop(0, rows // tile)
+            many = 4 * sub
+            base = own_rows if h is None else other_rows + ((place.y + h) % ny) * many
+            count = rows if h is None else many
+            tile = min(256, count)
+
+            @pl.loop(0, count // tile)
             def _(i):
                 n = pl.ds(pl.multiple_of(base + i * tile, tile), tile)
-                both = dot_nn(high[n, :], pt[...])
-                s = both[:, 0:group] + both[:, group : 2 * group] + dot_nn(low[n, :], pt[:, 0:group])
+                both = dot_nn(high[n, :], params[...])
+                s = both[:, 0:group] + both[:, group : 2 * group] + dot_nn(low[n, :], params[:, 0:group])
                 s = s.T
                 if not last:
                     scores[at, n] = s
@@ -449,7 +473,7 @@
     for c in range(2 * comps):
         total = total + stat[c, 1:2, :] * jnp.exp(stat[c, 0:1, :] - peak)
     norm[0:1, :] = peak + jnp.log(total)
-    loglik_ref[0:1, :] = norm[0:1, pl.ds(own_rows, rows)] - loglik_ref[0:1, :]
+    loglik_ref[...] = norm[0:1, pl.ds(own_rows, rows)] - loglik_ref[...]
 
     sums, lands, results = (sum_a, sum_b), (land_a, land_b), (first_ref, second_ref)
 
@@ -533,7 +557,7 @@
         out_shape=(
             jax.ShapeDtypeStruct((size, width), f32),
             jax.ShapeDtypeStruct((size, width + PAD), f32),
-            jax.ShapeDtypeStruct((8, rows), f32),
+            jax.ShapeDtypeStruct((1, rows), f32),
         ),
         in_specs=[pl.BlockSpec(memory_space=pl.ANY)] + [vmem] * 3,
         out_specs=(vmem, vmem, vmem),
@@ -543,7 +567,7 @@
             pltpu.VMEM((2 * comps, rows // comps // 2, width), f32),
             pltpu.VMEM((rows, width), f32),
             *[pltpu.VMEM((2 * rows, width), bf16)] * 4,
-            pltpu.VMEM((width, 2 * group), bf16),
+            pltpu.VMEM((2 * nx, width, 2 * group), bf16),
             pltpu.VMEM((count * size, 2 * rows), f32),
             pltpu.VMEM((2 * comps, 2, 2 * rows), f32),
             pltpu.VMEM((8, 2 * rows), f32),
@@ -565,7 +589,7 @@
     new_means = (first + means) / denom
     new_variances = (second[:, :width] + variances + means * means) / denom - new_means * new_means
     new_weights = counts / (rows * nx * nz)
-    return (new_means, new_variances, new_weights, loglik[0])
+    return (new_means, new_variances, new_weights, loglik.reshape(rows))
 
 
 def solution(mesh):

time: 140 us -> 129 us (0.921)
  Pallas kernels: 135 us -> 123 us
    pallas_call x1, Pallas kernels: 135 us -> 123 us  [per_device(): pl.pallas_call(functools.partial(kernel, nx, nz, comps), out_shape=(jax.S...]
where the time goes in v4:
time: 129 us; the launch traced here: 128 us
  Pallas kernels  123 us (95%)
  other arithmetic  3.11 us (2%)
    pallas_call x1, Pallas kernels, per_device(): pl.pallas_call(functools.partial(kernel, nx, nz, comps), out_shape=(jax.S...  123 us

profile of v4, /device:TPU:8, one launch (start us, length us, event | category | flops | bytes accessed | tf_op | source)
XLA Modules:
  0.0 128.0 jit_solution(17793509832260132718)
XLA Ops:
  0.6 0.0 copy-start.1
  0.6 0.0 copy-start
  0.7 123.0 %mixture.1 = (f32[32,1024]{1,0:T(8,128)}, f32[32,1152]{1,0:T(8,128)}, f32[1,1024]{1,0:T(1,128)}) custom-call(f32[1024,1024]{1,0:T(8,128)} %x_hbm.1, f32[32,1024]{1,0:T(8,128)} %means_ref.1, f32[32,1024]{1,0:T(8,128)} %var_ref.1, f32[1,32]{1,0:T(1,128)} %bitcast.3), custom_call_target="tpu_custom_call" | custom-call | tf_op jit(solution)/shard_map/mixture/pallas_call | solution.py:555
  123.6 1.3 %multiply_reduce_fusion = (f32[32]{0:T(128)}, f32[32]{0:T(128)S(1)}) fusion(f32[32,1152]{1,0:T(8,128)} %get-tuple-element.8), kind=kLoop, calls=%fused_computation.2 | loop fusion | flops 64 | bytes 384 | tf_op jit(solution)/shard_map/div | solution.py:591
  125.0 0.0 copy-done.1
  125.0 0.0 copy-done
  125.0 1.8 %multiply_subtract_fusion = (f32[32,1024]{1,0:T(8,128)}, f32[32,1024]{1,0:T(8,128)}) fusion(f32[32,1024]{1,0:T(8,128)S(1)} %copy-done, f32[32,1024]{1,0:T(8,128)S(1)} %copy-done.1, f32[32,1152]{1,0:T(8,128)} %get-tuple-element.8, f32[32]{0:T(128)S(1)} %get-tuple-element.11, f32[32,1024]{1,0:T(8,128)} %get-tuple-element.7), kind=kLoop, calls=%fused_computation | loop fusion | flops 262144 | bytes 786560 | tf_op jit(solution)/shard_map/sub | solution.py:590
  126.7 1.3 copy.9
Async XLA Ops:
  0.6 124.3 %copy-start.1 = (f32[32,1024]{1,0:T(8,128)S(1)}, f32[32,1024]{1,0:T(8,128)}, u32[]{:S(2)}) copy-start(f32[32,1024]{1,0:T(8,128)} %var_ref.1) | copy-start | bytes 393220
  0.6 124.3 %copy-start = (f32[32,1024]{1,0:T(8,128)S(1)}, f32[32,1024]{1,0:T(8,128)}, u32[]{:S(2)}) copy-start(f32[32,1024]{1,0:T(8,128)} %means_ref.1) | copy-start | bytes 393220

commit v5 on v4

--- a/solution.py
+++ b/solution.py
@@ -289,7 +289,7 @@
 
 
 def kernel(
-    nx, nz, comps, x_hbm, means_ref, var_ref, logw_ref, first_ref, second_ref, loglik_ref,
+    nx, nz, comps, x_hbm, means_ref, var_ref, logw_ref, new_means_ref, new_var_ref, weight_ref, loglik_ref,
     scaled, prec, other, x_ref, xh, xl, qh, ql, pt, scores, stat, norm, rh, rl,
     sum_a, sum_b, land_a, land_b,
     in_send, in_recv, out_send, out_recv, row_send, row_recv, stat_send, stat_recv, load_sem,
@@ -475,7 +475,7 @@
     norm[0:1, :] = peak + jnp.log(total)
     loglik_ref[...] = norm[0:1, pl.ds(own_rows, rows)] - loglik_ref[...]
 
-    sums, lands, results = (sum_a, sum_b), (land_a, land_b), (first_ref, second_ref)
+    sums, lands = (sum_a, sum_b), (land_a, land_b)
 
     def sum_copy(k, axis, way, slot):
         stream = OUT_STREAMS[k]
@@ -536,10 +536,15 @@
         for slot in cut:
             at = pl.ds(slot[2] * (size // 2), size // 2)
             out[index, at, lo:hi] = out[index, at, lo:hi] + land[landing(k, slot), at, lo:hi]
-        if (df, ds) == (0, 0):
-            results[stream[0]][:, lo:hi] = out[index, :, lo:hi]
         for axis, way, slot in reduce_sends(stream, df, ds, nf, ns):
             begin(sum_copy(k, axis, way, slot))
+    counts = sum_b[own, :, width : width + 1]
+    denom = counts + 1.0
+    means = means_ref[...]
+    new_means = (sum_a[own] + means) / denom
+    new_means_ref[...] = new_means
+    new_var_ref[...] = (sum_b[own, :, 0:width] + var_ref[...] + means * means) / denom - new_means * new_means
+    weight_ref[...] = jnp.sum(jnp.where(diagonal, counts, 0.0), axis=0, keepdims=True) / (rows * nx * place.full_z)
     for c in started:
         c.wait_send()
 
@@ -552,15 +557,16 @@
     vmem = pl.BlockSpec(memory_space=pltpu.VMEM)
     f32, bf16 = jnp.float32, jnp.bfloat16
     dma = pltpu.SemaphoreType.DMA
-    first, second, loglik = pl.pallas_call(
+    new_means, new_variances, new_weights, loglik = pl.pallas_call(
         functools.partial(kernel, nx, nz, comps),
         out_shape=(
             jax.ShapeDtypeStruct((size, width), f32),
-            jax.ShapeDtypeStruct((size, width + PAD), f32),
+            jax.ShapeDtypeStruct((size, width), f32),
+            jax.ShapeDtypeStruct((1, size), f32),
             jax.ShapeDtypeStruct((1, rows), f32),
         ),
         in_specs=[pl.BlockSpec(memory_space=pl.ANY)] + [vmem] * 3,
-        out_specs=(vmem, vmem, vmem),
+        out_specs=(vmem,) * 4,
         scratch_shapes=[
             pltpu.VMEM((count, size, width), f32),
             pltpu.VMEM((count, size, width + PAD), f32),
@@ -584,12 +590,7 @@
         ),
         name="mixture",
     )(x, means, variances, log_weights[None, :])
-    counts = second[:, width]
-    denom = (counts + 1.0)[:, None]
-    new_means = (first + means) / denom
-    new_variances = (second[:, :width] + variances + means * means) / denom - new_means * new_means
-    new_weights = counts / (rows * nx * nz)
-    return (new_means, new_variances, new_weights, loglik.reshape(rows))
+    return (new_means, new_variances, new_weights.reshape(size), loglik.reshape(rows))
 
 
 def solution(mesh):

time: 129 us -> 130 us (level)
  local copies, waits for them, and re-layouts: 1.28 us -> 5.49 us
  other arithmetic: 3.11 us -> 0 us
    unnamed x5 -> x4, local copies, waits for them, and re-layouts: 1.28 us -> 5.49 us
    sub x1 -> x0, other arithmetic: 1.76 us -> none  [per_device(): (second[:, :width] + variances + means * means) / denom]
    div x1 -> x0, other arithmetic: 1.34 us -> none  [per_device(): new_weights = counts / (rows * nx * nz)]
where the time goes in v5:
time: 130 us; the launch traced here: 129 us
  Pallas kernels  123 us (95%)
  local copies, waits for them, and re-layouts  5.49 us (4%)
    pallas_call x1, Pallas kernels, per_device(): pl.pallas_call(functools.partial(kernel, nx, nz, comps), out_shape=(jax.S...  123 us
    unnamed x4, local copies, waits for them, and re-layouts  5.49 us

profile of v5, /device:TPU:8, one launch (start us, length us, event | category | flops | bytes accessed | tf_op | source)
XLA Modules:
  0.0 129.1 jit_solution(10603095097806003194)
XLA Ops:
  0.6 123.0 %mixture.1 = (f32[32,1024]{1,0:T(8,128)}, f32[32,1024]{1,0:T(8,128)}, f32[1,32]{1,0:T(1,128)}, f32[1,1024]{1,0:T(1,128)}) custom-call(f32[1024,1024]{1,0:T(8,128)} %x_hbm.1, f32[32,1024]{1,0:T(8,128)} %means_ref.1, f32[32,1024]{1,0:T(8,128)} %var_ref.1, f32[1,32]{1,0:T(1,128)} %bitcast.4), custom_call_target="tpu_custom_call" | custom-call | tf_op jit(solution)/shard_map/mixture/pallas_call | solution.py:560
  123.6 1.6 %copy.12 = f32[32,1024]{1,0:T(8,128)} copy(f32[32,1024]{1,0:T(8,128)} %get-tuple-element.16) | data formatting | bytes 262144
  125.2 1.6 %copy.13 = f32[32,1024]{1,0:T(8,128)} copy(f32[32,1024]{1,0:T(8,128)} %get-tuple-element.17) | data formatting | bytes 262144
  126.8 1.1 copy.14
  127.9 1.3 copy.15
